TPU v7x, 32 devices: a whole 2x2x4 slice. The times are simulated.
32 devices in a mesh: row: 8 (over y, x, core), col: 4 (over z).
Axes of the slice: x: 2, y: 2, z: 4, core: 2. Of those that a mesh axis runs over, the one named last changes fastest.
Arguments:
- object_slices: float32 [2, 2, 1024, 512], P(None, None, 'row', 'col'), may hold values from -4 to 4
- probe: float32 [2, 128, 128], replicated, may hold values from -5 to 5
- phase: float32 [128, 128], replicated, may hold values from -3.140625 to 3.140625
- positions: int32 [8, 4, 4, 2], P('row', 'col'), may hold values from 0 to 127
- counts: int32 [8, 4], P('row', 'col'), may hold values from 1 to 4
- measured: float32 [8, 4, 4, 128, 128], P('row', 'col'), may hold values from 0.2 to 4
Outputs:
- updated: float32 [2, 2, 1024, 512], P(None, None, 'row', 'col')
Inputs may be any that keep to these rules, and one draw needn't show every extreme that they name: Slots k with k >= counts of the tile are padding and do not contribute. `positions`: a window may reach up to 127 pixels into the tiles below, to the right and diagonally below right.
All inputs are finite; a program needn't handle non-finite values.
Results may differ from a plain program's by a relative error of at most 0.0003.
Values sent between devices are 32-bit elements; how exact they have to be, the bound alone decides.
No kernel may reach another device: no remote copies, remote signals or barrier semaphores. Data moves between devices by JAX's collectives and lax.ppermute only.
A program may use at most 64 MiB of HBM per device.

v0:
```python
import functools

import jax
import jax.numpy as jnp
import ml_dtypes
import numpy as np
from jax import lax
from jax.experimental import pallas as pl
from jax.experimental.pallas import tpu as pltpu
from jax.sharding import PartitionSpec as P

ITERS = 2
step_rate = 0.02
F32 = jnp.float32
BF16 = jnp.bfloat16
VMEM = pl.BlockSpec(memory_space=pltpu.VMEM)
SMEM = pl.BlockSpec(memory_space=pltpu.SMEM)


def moved(value, rows, cols):
    nr, nc = lax.axis_size("row"), lax.axis_size("col")
    pairs = [
        (r * nc + c, ((r + rows) % nr) * nc + (c + cols) % nc)
        for r in range(nr)
        for c in range(nc)
    ]
    return lax.ppermute(value, ("row", "col"), pairs)


def dft_tables(width):
    index = np.arange(width)
    angle = (index[:, None] * index[None, :] % width) * (-2.0 * np.pi / width)
    cos, sin = np.cos(angle) / np.sqrt(width), np.sin(angle) / np.sqrt(width)
    right = np.block([[cos, sin], [-sin, cos]]).astype(np.float32)
    left = np.block([[cos, -sin], [sin, cos]]).astype(np.float32)
    tables = []
    for table in (right, left):
        high = table.astype(ml_dtypes.bfloat16)
        low = (table - high.astype(np.float32)).astype(ml_dtypes.bfloat16)
        tables += [high, low]
    return [jnp.asarray(t) for t in tables]


def halves(x):
    high = x.astype(BF16)
    low = (x - high.astype(F32)).astype(BF16)
    return high, low


def dot3(a, b):
    (ah, al), (bh, bl) = a, b
    mm = functools.partial(jnp.dot, preferred_element_type=F32)
    return mm(ah, bh) + mm(al, bh) + mm(ah, bl)


def along_lanes(z, table):
    n = z[0][0].shape[0]
    x = jnp.concatenate([jnp.concatenate(s, axis=1) for s in z], axis=0)
    y = dot3(halves(x), table)
    return [(y[k * n : (k + 1) * n, :n], y[k * n : (k + 1) * n, n:]) for k in range(2)]


def along_rows(z, table):
    n = z[0][0].shape[0]
    x = jnp.concatenate(
        [jnp.concatenate([s[part] for s in z], axis=1) for part in range(2)], axis=0
    )
    y = dot3(table, halves(x))
    return [(y[:n, k * n : (k + 1) * n], y[n:, k * n : (k + 1) * n]) for k in range(2)]


def times(a, b):
    return (a[0] * b[0] - a[1] * b[1], a[0] * b[1] + a[1] * b[0])


def times_conj(a, b):
    return (a[0] * b[0] + a[1] * b[1], a[1] * b[0] - a[0] * b[1])


def own_masks(positions, slot, width):
    rows = lax.broadcasted_iota(jnp.int32, (width, width), 0)
    cols = lax.broadcasted_iota(jnp.int32, (width, width), 1)
    return rows >= positions[2 * slot], cols >= positions[2 * slot + 1]


def window(tiles, masks, part):
    t00, t01, t10, t11 = (t[part] for t in tiles)
    rm, cm = masks
    return jnp.where(rm, jnp.where(cm, t00, t01), jnp.where(cm, t10, t11))


def scatter(outs, masks, g, first):
    rm, cm = masks
    for part in range(2):
        top = jnp.where(rm, g[part], 0.0)
        low = jnp.where(rm, 0.0, g[part])
        for ref, value in zip(
            outs,
            (
                jnp.where(cm, top, 0.0),
                jnp.where(cm, 0.0, top),
                jnp.where(cm, low, 0.0),
                jnp.where(cm, 0.0, low),
            ),
        ):
            if first:
                ref[part] = value
            else:
                ref[part] += value


def prepare_kernel(positions, probe, phase, rolled, prop):
    for slot in range(rolled.shape[0]):
        for part in range(2):
            x = pltpu.roll(probe[part], positions[2 * slot], 0)
            rolled[slot, part] = pltpu.roll(x, positions[2 * slot + 1], 1)
    prop[0] = jnp.cos(phase[...])
    prop[1] = jnp.sin(phase[...])


def first_slice_kernel(positions, rolled, t00, t01, t10, t11, prop, rh, rl, lh, ll, wave):
    right, left = (rh[...], rl[...]), (lh[...], ll[...])
    width = prop.shape[-1]
    tiles = (t00, t01, t10, t11)
    h = (prop[0], prop[1])
    for pair in range(0, rolled.shape[0], 2):
        z = []
        for slot in (pair, pair + 1):
            masks = own_masks(positions, slot, width)
            w = [window(tiles, masks, part) for part in range(2)]
            z.append(times((rolled[slot, 0], rolled[slot, 1]), w))
        z = along_rows(along_lanes(z, right), left)
        z = [times(s, h) for s in z]
        z = along_lanes(along_rows(z, right), left)
        for k in range(2):
            wave[pair + k, 0], wave[pair + k, 1] = z[k]


def second_slice_kernel(
    positions, counts, wave, t00, t01, t10, t11, measured, rh, rl, lh, ll, g00, g01, g10, g11, back
):
    right, left = (rh[...], rl[...]), (lh[...], ll[...])
    width = measured.shape[-1]
    tiles = (t00, t01, t10, t11)
    for pair in range(0, wave.shape[0], 2):
        z = []
        for slot in (pair, pair + 1):
            masks = own_masks(positions, slot, width)
            w = [window(tiles, masks, part) for part in range(2)]
            z.append(times((wave[slot, 0], wave[slot, 1]), w))
        z = along_rows(along_lanes(z, right), left)
        g = []
        for k in range(2):
            re, im = z[k]
            live = (pair + k < counts[0]).astype(F32)
            pull = (re * re + im * im - measured[pair + k]) * (2.0 * live)
            g.append((pull * re, pull * im))
        g = along_lanes(along_rows(g, right), left)
        for k in range(2):
            slot = pair + k
            masks = own_masks(positions, slot, width)
            w = [window(tiles, masks, part) for part in range(2)]
            scatter(
                (g00, g01, g10, g11),
                masks,
                times_conj(g[k], (wave[slot, 0], wave[slot, 1])),
                slot == 0,
            )
            back[slot, 0], back[slot, 1] = times_conj(g[k], w)


def first_back_kernel(positions, back, rolled, prop, rh, rl, lh, ll, g00, g01, g10, g11):
    right, left = (rh[...], rl[...]), (lh[...], ll[...])
    width = prop.shape[-1]
    h = (prop[0], prop[1])
    for pair in range(0, rolled.shape[0], 2):
        z = [(back[slot, 0], back[slot, 1]) for slot in (pair, pair + 1)]
        z = along_rows(along_lanes(z, right), left)
        z = [times_conj(s, h) for s in z]
        z = along_lanes(along_rows(z, right), left)
        for k in range(2):
            slot = pair + k
            masks = own_masks(positions, slot, width)
            scatter(
                (g00, g01, g10, g11),
                masks,
                times_conj(z[k], (rolled[slot, 0], rolled[slot, 1])),
                slot == 0,
            )


def update_kernel(tile, own, right, below, corner, out):
    out[...] = tile[...] - step_rate * (own[...] + right[...] + below[...] + corner[...])


def call(kernel, ins, outs, args, name):
    return pl.pallas_call(
        kernel,
        out_shape=outs,
        in_specs=ins,
        out_specs=[VMEM] * len(outs) if isinstance(outs, (list, tuple)) else VMEM,
        name=name,
    )(*args)


def per_device(object_slices, probe, phase, positions, counts, measured):
    width = probe.shape[-1]
    assert object_slices.shape[-1] == width and object_slices.shape[-2] == width
    corners = positions.reshape(-1)
    slots = positions.shape[2]
    live = counts.reshape(-1)
    intensity = measured[0, 0]
    tables = dft_tables(width)
    plane = jax.ShapeDtypeStruct((2, width, width), F32)
    stack = jax.ShapeDtypeStruct((slots, 2, width, width), F32)

    rolled, prop = call(
        prepare_kernel, [SMEM, VMEM, VMEM], [stack, plane], (corners, probe, phase), "prepare"
    )

    def fetch(tile):
        return tile, moved(tile, 0, -1), moved(tile, -1, 0), moved(tile, -1, -1)

    def returned(g):
        return g[0], moved(g[1], 0, 1), moved(g[2], 1, 0), moved(g[3], 1, 1)

    def update(tile, g):
        return call(update_kernel, [VMEM] * 5, plane, (tile, *g), "update")

    first, second = object_slices[0], object_slices[1]
    for _ in range(ITERS):
        tiles0 = fetch(first)
        tiles1 = fetch(second)
        wave = call(
            first_slice_kernel,
            [SMEM] + [VMEM] * 10,
            stack,
            (corners, rolled, *tiles0, prop, *tables),
            "first",
        )
        *g1, back = call(
            second_slice_kernel,
            [SMEM] * 2 + [VMEM] * 10,
            [plane] * 4 + [stack],
            (corners, live, wave, *tiles1, intensity, *tables),
            "second",
        )
        g1 = returned(g1)
        g0 = call(
            first_back_kernel,
            [SMEM] + [VMEM] * 7,
            [plane] * 4,
            (corners, back, rolled, prop, *tables),
            "back",
        )
        g0 = returned(g0)
        second = update(second, g1)
        first = update(first, g0)
    return jnp.stack([first, second])


def solution(mesh):
    return jax.shard_map(
        per_device,
        mesh=mesh,
        in_specs=(
            P(None, None, "row", "col"),
            P(),
            P(),
            P("row", "col", None, None),
            P("row", "col"),
            P("row", "col", None, None, None),
        ),
        out_specs=P(None, None, "row", "col"),
        check_vma=False,
    )
```

profile of v0, /device:TPU:0, one launch (start us, length us, event | category | flops | bytes accessed | tf_op | source)
XLA Modules:
  0.0 93.9 jit_solution(7273500128726042009)
XLA Ops:
  1.0 6.5 %collective-permute-start.2 = (f32[2,128,128]{2,1,0:T(8,128)S(1)}, f32[2,128,128]{2,1,0:T(8,128)S(1)}, u32[]{:S(2)}, u32[]{:S(2)}) collective-permute-start(f32[2,128,128]{2,1,0:T(8,128)S(1)} %get-tuple-element.45.t00.tile), channel_id=1, source_target_pairs={{0,31},{1,28},{2,29},{3,30},{4,3},{5,0},{6,1},{7,2},{8,7},{9,4},{1... | collective-permute-start | bytes 393224 | tf_op jit(solution)/shard_map/ppermute | solution.py:27
  9.5 1.9 %collective-permute-done.2.t11 = f32[2,128,128]{2,1,0:T(8,128)S(1)} collective-permute-done((f32[2,128,128]{2,1,0:T(8,128)S(1)}, f32[2,128,128]{2,1,0:T(8,128)S(1)}, u32[]{:S(2)}, u32[]{:S(2)}) %collective-permute-start.2) | collective-permute-done | bytes 131104 | tf_op jit(solution)/shard_map/ppermute | solution.py:27
  13.7 2.1 %prepare.1 = (f32[4,2,128,128]{3,2,1,0:T(8,128)}, f32[2,128,128]{2,1,0:T(8,128)}) custom-call(s32[8]{0:T(128)} %reshape.6.positions, f32[2,128,128]{2,1,0:T(8,128)} %probe.1, f32[128,128]{1,0:T(8,128)} %phase.1), custom_call_target="tpu_custom_call" | custom-call | tf_op jit(solution)/shard_map/prepare/pallas_call | solution.py:197
  16.5 4.5 %first.2.wave = f32[4,2,128,128]{3,2,1,0:T(8,128)} custom-call(s32[8]{0:T(128)} %reshape.6.positions, f32[4,2,128,128]{3,2,1,0:T(8,128)} %get-tuple-element.25.rolled, f32[2,128,128]{2,1,0:T(8,128)} %copy-done.1, f32[2,128,128]{2,1,0:T(8,128)} %copy-done.13, f32[2,128,128]{2,1,0:T(8,128)} %copy-done.10, f32[2,128,128]{2,1,0:T(8,128)} %copy-done.7, ...), custom_call_target="tpu_custom_call" | custom-call | tf_op jit(solution)/shard_map/first/pallas_call | solution.py:197
  21.8 4.8 %second.2 = (f32[2,128,128]{2,1,0:T(8,128)}, f32[2,128,128]{2,1,0:T(8,128)}, f32[2,128,128]{2,1,0:T(8,128)}, f32[2,128,128]{2,1,0:T(8,128)}, f32[4,2,128,128]{3,2,1,0:T(8,128)}) custom-call(s32[8]{0:T(128)} %reshape.6.positions, s32[1]{0:T(128)} %bitcast.8.counts, f32[4,2,128,128]{3,2,1,0:T(8,128)} %first.2.wave, f32[2,128,128]{2,1,0:T(8,128)} %copy-done, ...), custom_call_target="tpu_custom_call" | custom-call | tf_op jit(solution)/shard_map/second/pallas_call | solution.py:197
  26.7 4.5 %back.2 = (f32[2,128,128]{2,1,0:T(8,128)}, f32[2,128,128]{2,1,0:T(8,128)}, f32[2,128,128]{2,1,0:T(8,128)}, f32[2,128,128]{2,1,0:T(8,128)}) custom-call(s32[8]{0:T(128)} %reshape.6.positions, f32[4,2,128,128]{3,2,1,0:T(8,128)} %get-tuple-element.27.back, f32[4,2,128,128]{3,2,1,0:T(8,128)} %get-tuple-element.25.rolled, f32[2,128,128]{2,1,0:T(8,128)} %get-tuple-element.26.prop, ...), custom_call_target="tpu_custom_call" | custom-call | tf_op jit(solution)/shard_map/back/pallas_call | solution.py:197
  33.1 1.8 %collective-permute-start.12 = (f32[2,128,128]{2,1,0:T(8,128)S(1)}, f32[2,128,128]{2,1,0:T(8,128)S(1)}, u32[]{:S(2)}, u32[]{:S(2)}) collective-permute-start(f32[2,128,128]{2,1,0:T(8,128)S(1)} %copy-done.32), channel_id=1, source_target_pairs={{0,1},{1,2},{2,3},{3,0},{4,5},{5,6},{6,7},{7,4},{8,9},{9,10},{10,1... | collective-permute-start | bytes 393224 | tf_op jit(solution)/shard_map/ppermute | solution.py:27
  35.8 2.9 %collective-permute-done.6.right = f32[2,128,128]{2,1,0:T(8,128)S(1)} collective-permute-done((f32[2,128,128]{2,1,0:T(8,128)}, f32[2,128,128]{2,1,0:T(8,128)S(1)}, u32[]{:S(2)}, u32[]{:S(2)}) %collective-permute-start.6) | collective-permute-done | bytes 131104 | tf_op jit(solution)/shard_map/ppermute | solution.py:27
  39.5 6.5 %collective-permute-done.8.corner = f32[2,128,128]{2,1,0:T(8,128)S(1)} collective-permute-done((f32[2,128,128]{2,1,0:T(8,128)}, f32[2,128,128]{2,1,0:T(8,128)S(1)}, u32[]{:S(2)}, u32[]{:S(2)}) %collective-permute-start.8) | collective-permute-done | bytes 131104 | tf_op jit(solution)/shard_map/ppermute | solution.py:27
  46.7 1.9 %update.4.t00.tile = f32[2,128,128]{2,1,0:T(8,128)} custom-call(f32[2,128,128]{2,1,0:T(8,128)} %copy-done.1, f32[2,128,128]{2,1,0:T(8,128)} %get-tuple-element.28.own, f32[2,128,128]{2,1,0:T(8,128)} %copy-done.20, f32[2,128,128]{2,1,0:T(8,128)} %copy-done.22, f32[2,128,128]{2,1,0:T(8,128)} %copy-done.25), custom_call_target="tpu_custom_call" | custom-call | tf_op jit(solution)/shard_map/update/pallas_call | solution.py:197
  48.5 1.1 %collective-permute-start.10 = (f32[2,128,128]{2,1,0:T(8,128)}, f32[2,128,128]{2,1,0:T(8,128)S(1)}, u32[]{:S(2)}, u32[]{:S(2)}) collective-permute-start(f32[2,128,128]{2,1,0:T(8,128)} %update.4.t00.tile), channel_id=1, source_target_pairs={{0,28},{1,29},{2,30},{3,31},{4,0},{5,1},{6,2},{7,3},{8,4},{9,5},{1... | collective-permute-start | bytes 393224 | tf_op jit(solution)/shard_map/ppermute | solution.py:27
  49.7 1.8 %collective-permute-done.14.corner = f32[2,128,128]{2,1,0:T(8,128)S(1)} collective-permute-done((f32[2,128,128]{2,1,0:T(8,128)S(1)}, f32[2,128,128]{2,1,0:T(8,128)S(1)}, u32[]{:S(2)}, u32[]{:S(2)}) %collective-permute-start.14) | collective-permute-done | bytes 131104 | tf_op jit(solution)/shard_map/ppermute | solution.py:27
  52.1 1.8 %update.5.t00.tile = f32[2,128,128]{2,1,0:T(8,128)} custom-call(f32[2,128,128]{2,1,0:T(8,128)} %copy-done, f32[2,128,128]{2,1,0:T(8,128)} %get-tuple-element.32.own, f32[2,128,128]{2,1,0:T(8,128)} %copy-done.15, f32[2,128,128]{2,1,0:T(8,128)} %copy-done.16, f32[2,128,128]{2,1,0:T(8,128)} %copy-done.17), custom_call_target="tpu_custom_call" | custom-call | tf_op jit(solution)/shard_map/update/pallas_call | solution.py:197
  54.5 3.0 %collective-permute-start.15 = (f32[2,128,128]{2,1,0:T(8,128)}, f32[2,128,128]{2,1,0:T(8,128)S(1)}, u32[]{:S(2)}, u32[]{:S(2)}) collective-permute-start(f32[2,128,128]{2,1,0:T(8,128)} %update.5.t00.tile), channel_id=1, source_target_pairs={{0,3},{1,0},{2,1},{3,2},{4,7},{5,4},{6,5},{7,6},{8,11},{9,8},{10,9... | collective-permute-start | bytes 393224 | tf_op jit(solution)/shard_map/ppermute | solution.py:27
  58.7 4.5 %first.3.wave = f32[4,2,128,128]{3,2,1,0:T(8,128)} custom-call(s32[8]{0:T(128)} %reshape.6.positions, f32[4,2,128,128]{3,2,1,0:T(8,128)} %get-tuple-element.25.rolled, f32[2,128,128]{2,1,0:T(8,128)} %update.4.t00.tile, f32[2,128,128]{2,1,0:T(8,128)} %copy-done.8, f32[2,128,128]{2,1,0:T(8,128)} %copy-done.4, f32[2,128,128]{2,1,0:T(8,128)} %copy-done.3, ...), custom_call_target="tpu_custom_call" | custom-call | tf_op jit(solution)/shard_map/first/pallas_call | solution.py:197
  64.0 4.8 %second.3 = (f32[2,128,128]{2,1,0:T(8,128)}, f32[2,128,128]{2,1,0:T(8,128)}, f32[2,128,128]{2,1,0:T(8,128)}, f32[2,128,128]{2,1,0:T(8,128)}, f32[4,2,128,128]{3,2,1,0:T(8,128)}) custom-call(s32[8]{0:T(128)} %reshape.6.positions, s32[1]{0:T(128)} %bitcast.9.counts, f32[4,2,128,128]{3,2,1,0:T(8,128)} %first.3.wave, f32[2,128,128]{2,1,0:T(8,128)} %update.5.t00.tile, ...), custom_call_target="tpu_custom_call" | custom-call | tf_op jit(solution)/shard_map/second/pallas_call | solution.py:197
  68.9 4.5 %back.3 = (f32[2,128,128]{2,1,0:T(8,128)}, f32[2,128,128]{2,1,0:T(8,128)}, f32[2,128,128]{2,1,0:T(8,128)}, f32[2,128,128]{2,1,0:T(8,128)}) custom-call(s32[8]{0:T(128)} %reshape.6.positions, f32[4,2,128,128]{3,2,1,0:T(8,128)} %get-tuple-element.36.back, f32[4,2,128,128]{3,2,1,0:T(8,128)} %get-tuple-element.25.rolled, f32[2,128,128]{2,1,0:T(8,128)} %get-tuple-element.26.prop, ...), custom_call_target="tpu_custom_call" | custom-call | tf_op jit(solution)/shard_map/back/pallas_call | solution.py:197
  73.4 2.0 %collective-permute-start.20 = (f32[2,128,128]{2,1,0:T(8,128)}, f32[2,128,128]{2,1,0:T(8,128)S(1)}, u32[]{:S(2)}, u32[]{:S(2)}) collective-permute-start(f32[2,128,128]{2,1,0:T(8,128)} %get-tuple-element.40), channel_id=1, source_target_pairs={{0,5},{1,6},{2,7},{3,4},{4,9},{5,10},{6,11},{7,8},{8,13},{9,14},{1... | collective-permute-start | bytes 393224 | tf_op jit(solution)/shard_map/ppermute | solution.py:27
  76.3 5.4 %collective-permute-done.18.right = f32[2,128,128]{2,1,0:T(8,128)S(1)} collective-permute-done((f32[2,128,128]{2,1,0:T(8,128)}, f32[2,128,128]{2,1,0:T(8,128)S(1)}, u32[]{:S(2)}, u32[]{:S(2)}) %collective-permute-start.18) | collective-permute-done | bytes 131104 | tf_op jit(solution)/shard_map/ppermute | solution.py:27
  81.8 2.0 %collective-permute-done.20.corner = f32[2,128,128]{2,1,0:T(8,128)S(1)} collective-permute-done((f32[2,128,128]{2,1,0:T(8,128)}, f32[2,128,128]{2,1,0:T(8,128)S(1)}, u32[]{:S(2)}, u32[]{:S(2)}) %collective-permute-start.20) | collective-permute-done | bytes 131104 | tf_op jit(solution)/shard_map/ppermute | solution.py:27
  84.4 1.8 %update.6 = f32[2,128,128]{2,1,0:T(8,128)} custom-call(f32[2,128,128]{2,1,0:T(8,128)} %update.4.t00.tile, f32[2,128,128]{2,1,0:T(8,128)} %get-tuple-element.37.own, f32[2,128,128]{2,1,0:T(8,128)} %copy-done.21, f32[2,128,128]{2,1,0:T(8,128)} %copy-done.23, f32[2,128,128]{2,1,0:T(8,128)} %copy-done.26), custom_call_target="tpu_custom_call" | custom-call | tf_op jit(solution)/shard_map/update/pallas_call | solution.py:197
  86.2 3.5 %collective-permute-done.23.corner = f32[2,128,128]{2,1,0:T(8,128)S(1)} collective-permute-done((f32[2,128,128]{2,1,0:T(8,128)S(1)}, f32[2,128,128]{2,1,0:T(8,128)S(1)}, u32[]{:S(2)}, u32[]{:S(2)}) %collective-permute-start.23) | collective-permute-done | bytes 131104 | tf_op jit(solution)/shard_map/ppermute | solution.py:27
  90.4 1.9 %update.7 = f32[2,128,128]{2,1,0:T(8,128)} custom-call(f32[2,128,128]{2,1,0:T(8,128)} %update.5.t00.tile, f32[2,128,128]{2,1,0:T(8,128)} %get-tuple-element.41.own, f32[2,128,128]{2,1,0:T(8,128)} %copy-done.18, f32[2,128,128]{2,1,0:T(8,128)} %copy-done.19, f32[2,128,128]{2,1,0:T(8,128)} %copy-done.24), custom_call_target="tpu_custom_call" | custom-call | tf_op jit(solution)/shard_map/update/pallas_call | solution.py:197
  92.3 1.6 %pad_maximum_fusion = f32[2,2,128,128]{3,2,1,0:T(8,128)} fusion(f32[1,2,128,128]{3,2,1,0:T(8,128)} %bitcast.13, f32[1,2,128,128]{3,2,1,0:T(8,128)S(1)} %bitcast.12), kind=kLoop, calls=%fused_computation | loop fusion | flops 65536 | bytes 524288 | tf_op jit(solution)/shard_map/stack | solution.py:259
  (107 shorter events, 15.8 us)
Async XLA Ops:
  1.0 10.3 %collective-permute-start.2 = (f32[2,128,128]{2,1,0:T(8,128)S(1)}, f32[2,128,128]{2,1,0:T(8,128)S(1)}, u32[]{:S(2)}, u32[]{:S(2)}) collective-permute-start(f32[2,128,128]{2,1,0:T(8,128)S(1)} %get-tuple-element.45.t00.tile), channel_id=1, source_target_pairs={{0,31},{1,28},{2,29},{3,30},{4,3},{5,0},{6,1},{7,2},{8,7},{9,4},{1... | collective-permute-start | bytes 393224 | tf_op jit(solution)/shard_map/ppermute | solution.py:27
  7.5 8.4 %collective-permute-start.1 = (f32[2,128,128]{2,1,0:T(8,128)S(1)}, f32[2,128,128]{2,1,0:T(8,128)S(1)}, u32[]{:S(2)}, u32[]{:S(2)}) collective-permute-start(f32[2,128,128]{2,1,0:T(8,128)S(1)} %get-tuple-element.45.t00.tile), channel_id=1, source_target_pairs={{0,28},{1,29},{2,30},{3,31},{4,0},{5,1},{6,2},{7,3},{8,4},{9,5},{1... | collective-permute-start | bytes 393224 | tf_op jit(solution)/shard_map/ppermute | solution.py:27
  8.3 7.5 %collective-permute-start = (f32[2,128,128]{2,1,0:T(8,128)S(1)}, f32[2,128,128]{2,1,0:T(8,128)S(1)}, u32[]{:S(2)}, u32[]{:S(2)}) collective-permute-start(f32[2,128,128]{2,1,0:T(8,128)S(1)} %get-tuple-element.45.t00.tile), channel_id=1, source_target_pairs={{0,3},{1,0},{2,1},{3,2},{4,7},{5,4},{6,5},{7,6},{8,11},{9,8},{10,9... | collective-permute-start | bytes 393224 | tf_op jit(solution)/shard_map/ppermute | solution.py:27
  8.8 12.3 %collective-permute-start.5 = (f32[2,128,128]{2,1,0:T(8,128)S(1)}, f32[2,128,128]{2,1,0:T(8,128)S(1)}, u32[]{:S(2)}, u32[]{:S(2)}) collective-permute-start(f32[2,128,128]{2,1,0:T(8,128)S(1)} %get-tuple-element.46.t00.tile), channel_id=1, source_target_pairs={{0,31},{1,28},{2,29},{3,30},{4,3},{5,0},{6,1},{7,2},{8,7},{9,4},{1... | collective-permute-start | bytes 393224 | tf_op jit(solution)/shard_map/ppermute | solution.py:27
  8.8 12.3 %collective-permute-start.4 = (f32[2,128,128]{2,1,0:T(8,128)S(1)}, f32[2,128,128]{2,1,0:T(8,128)S(1)}, u32[]{:S(2)}, u32[]{:S(2)}) collective-permute-start(f32[2,128,128]{2,1,0:T(8,128)S(1)} %get-tuple-element.46.t00.tile), channel_id=1, source_target_pairs={{0,28},{1,29},{2,30},{3,31},{4,0},{5,1},{6,2},{7,3},{8,4},{9,5},{1... | collective-permute-start | bytes 393224 | tf_op jit(solution)/shard_map/ppermute | solution.py:27
  11.4 9.7 %collective-permute-start.3 = (f32[2,128,128]{2,1,0:T(8,128)S(1)}, f32[2,128,128]{2,1,0:T(8,128)S(1)}, u32[]{:S(2)}, u32[]{:S(2)}) collective-permute-start(f32[2,128,128]{2,1,0:T(8,128)S(1)} %get-tuple-element.46.t00.tile), channel_id=1, source_target_pairs={{0,3},{1,0},{2,1},{3,2},{4,7},{5,4},{6,5},{7,6},{8,11},{9,8},{10,9... | collective-permute-start | bytes 393224 | tf_op jit(solution)/shard_map/ppermute | solution.py:27
  31.2 7.5 %collective-permute-start.6 = (f32[2,128,128]{2,1,0:T(8,128)}, f32[2,128,128]{2,1,0:T(8,128)S(1)}, u32[]{:S(2)}, u32[]{:S(2)}) collective-permute-start(f32[2,128,128]{2,1,0:T(8,128)} %get-tuple-element.29), channel_id=1, source_target_pairs={{0,1},{1,2},{2,3},{3,0},{4,5},{5,6},{6,7},{7,4},{8,9},{9,10},{10,1... | collective-permute-start | bytes 393224 | tf_op jit(solution)/shard_map/ppermute | solution.py:27
  32.2 7.3 %collective-permute-start.7 = (f32[2,128,128]{2,1,0:T(8,128)}, f32[2,128,128]{2,1,0:T(8,128)S(1)}, u32[]{:S(2)}, u32[]{:S(2)}) collective-permute-start(f32[2,128,128]{2,1,0:T(8,128)} %get-tuple-element.30), channel_id=1, source_target_pairs={{0,4},{1,5},{2,6},{3,7},{4,8},{5,9},{6,10},{7,11},{8,12},{9,13},{1... | collective-permute-start | bytes 393224 | tf_op jit(solution)/shard_map/ppermute | solution.py:27
  33.0 13.0 %collective-permute-start.8 = (f32[2,128,128]{2,1,0:T(8,128)}, f32[2,128,128]{2,1,0:T(8,128)S(1)}, u32[]{:S(2)}, u32[]{:S(2)}) collective-permute-start(f32[2,128,128]{2,1,0:T(8,128)} %get-tuple-element.31), channel_id=1, source_target_pairs={{0,5},{1,6},{2,7},{3,4},{4,9},{5,10},{6,11},{7,8},{8,13},{9,14},{1... | collective-permute-start | bytes 393224 | tf_op jit(solution)/shard_map/ppermute | solution.py:27
  33.1 16.5 %collective-permute-start.12 = (f32[2,128,128]{2,1,0:T(8,128)S(1)}, f32[2,128,128]{2,1,0:T(8,128)S(1)}, u32[]{:S(2)}, u32[]{:S(2)}) collective-permute-start(f32[2,128,128]{2,1,0:T(8,128)S(1)} %copy-done.32), channel_id=1, source_target_pairs={{0,1},{1,2},{2,3},{3,0},{4,5},{5,6},{6,7},{7,4},{8,9},{9,10},{10,1... | collective-permute-start | bytes 393224 | tf_op jit(solution)/shard_map/ppermute | solution.py:27
  34.9 14.7 %collective-permute-start.13 = (f32[2,128,128]{2,1,0:T(8,128)S(1)}, f32[2,128,128]{2,1,0:T(8,128)S(1)}, u32[]{:S(2)}, u32[]{:S(2)}) collective-permute-start(f32[2,128,128]{2,1,0:T(8,128)S(1)} %copy-done.29), channel_id=1, source_target_pairs={{0,4},{1,5},{2,6},{3,7},{4,8},{5,9},{6,10},{7,11},{8,12},{9,13},{1... | collective-permute-start | bytes 393224 | tf_op jit(solution)/shard_map/ppermute | solution.py:27
  38.7 12.8 %collective-permute-start.14 = (f32[2,128,128]{2,1,0:T(8,128)S(1)}, f32[2,128,128]{2,1,0:T(8,128)S(1)}, u32[]{:S(2)}, u32[]{:S(2)}) collective-permute-start(f32[2,128,128]{2,1,0:T(8,128)S(1)} %copy-done.28), channel_id=1, source_target_pairs={{0,5},{1,6},{2,7},{3,4},{4,9},{5,10},{6,11},{7,8},{8,13},{9,14},{1... | collective-permute-start | bytes 393224 | tf_op jit(solution)/shard_map/ppermute | solution.py:27
  48.5 5.9 %collective-permute-start.11 = (f32[2,128,128]{2,1,0:T(8,128)}, f32[2,128,128]{2,1,0:T(8,128)S(1)}, u32[]{:S(2)}, u32[]{:S(2)}) collective-permute-start(f32[2,128,128]{2,1,0:T(8,128)} %update.4.t00.tile), channel_id=1, source_target_pairs={{0,31},{1,28},{2,29},{3,30},{4,3},{5,0},{6,1},{7,2},{8,7},{9,4},{1... | collective-permute-start | bytes 393224 | tf_op jit(solution)/shard_map/ppermute | solution.py:27
  48.5 8.9 %collective-permute-start.10 = (f32[2,128,128]{2,1,0:T(8,128)}, f32[2,128,128]{2,1,0:T(8,128)S(1)}, u32[]{:S(2)}, u32[]{:S(2)}) collective-permute-start(f32[2,128,128]{2,1,0:T(8,128)} %update.4.t00.tile), channel_id=1, source_target_pairs={{0,28},{1,29},{2,30},{3,31},{4,0},{5,1},{6,2},{7,3},{8,4},{9,5},{1... | collective-permute-start | bytes 393224 | tf_op jit(solution)/shard_map/ppermute | solution.py:27
  49.6 7.8 %collective-permute-start.9 = (f32[2,128,128]{2,1,0:T(8,128)}, f32[2,128,128]{2,1,0:T(8,128)S(1)}, u32[]{:S(2)}, u32[]{:S(2)}) collective-permute-start(f32[2,128,128]{2,1,0:T(8,128)} %update.4.t00.tile), channel_id=1, source_target_pairs={{0,3},{1,0},{2,1},{3,2},{4,7},{5,4},{6,5},{7,6},{8,11},{9,8},{10,9... | collective-permute-start | bytes 393224 | tf_op jit(solution)/shard_map/ppermute | solution.py:27
  54.0 9.3 %collective-permute-start.17 = (f32[2,128,128]{2,1,0:T(8,128)}, f32[2,128,128]{2,1,0:T(8,128)S(1)}, u32[]{:S(2)}, u32[]{:S(2)}) collective-permute-start(f32[2,128,128]{2,1,0:T(8,128)} %update.5.t00.tile), channel_id=1, source_target_pairs={{0,31},{1,28},{2,29},{3,30},{4,3},{5,0},{6,1},{7,2},{8,7},{9,4},{1... | collective-permute-start | bytes 393224 | tf_op jit(solution)/shard_map/ppermute | solution.py:27
  54.0 9.3 %collective-permute-start.16 = (f32[2,128,128]{2,1,0:T(8,128)}, f32[2,128,128]{2,1,0:T(8,128)S(1)}, u32[]{:S(2)}, u32[]{:S(2)}) collective-permute-start(f32[2,128,128]{2,1,0:T(8,128)} %update.5.t00.tile), channel_id=1, source_target_pairs={{0,28},{1,29},{2,30},{3,31},{4,0},{5,1},{6,2},{7,3},{8,4},{9,5},{1... | collective-permute-start | bytes 393224 | tf_op jit(solution)/shard_map/ppermute | solution.py:27
  54.5 8.8 %collective-permute-start.15 = (f32[2,128,128]{2,1,0:T(8,128)}, f32[2,128,128]{2,1,0:T(8,128)S(1)}, u32[]{:S(2)}, u32[]{:S(2)}) collective-permute-start(f32[2,128,128]{2,1,0:T(8,128)} %update.5.t00.tile), channel_id=1, source_target_pairs={{0,3},{1,0},{2,1},{3,2},{4,7},{5,4},{6,5},{7,6},{8,11},{9,8},{10,9... | collective-permute-start | bytes 393224 | tf_op jit(solution)/shard_map/ppermute | solution.py:27
  73.4 8.4 %collective-permute-start.18 = (f32[2,128,128]{2,1,0:T(8,128)}, f32[2,128,128]{2,1,0:T(8,128)S(1)}, u32[]{:S(2)}, u32[]{:S(2)}) collective-permute-start(f32[2,128,128]{2,1,0:T(8,128)} %get-tuple-element.38), channel_id=1, source_target_pairs={{0,1},{1,2},{2,3},{3,0},{4,5},{5,6},{6,7},{7,4},{8,9},{9,10},{10,1... | collective-permute-start | bytes 393224 | tf_op jit(solution)/shard_map/ppermute | solution.py:27
  73.4 8.4 %collective-permute-start.19 = (f32[2,128,128]{2,1,0:T(8,128)}, f32[2,128,128]{2,1,0:T(8,128)S(1)}, u32[]{:S(2)}, u32[]{:S(2)}) collective-permute-start(f32[2,128,128]{2,1,0:T(8,128)} %get-tuple-element.39), channel_id=1, source_target_pairs={{0,4},{1,5},{2,6},{3,7},{4,8},{5,9},{6,10},{7,11},{8,12},{9,13},{1... | collective-permute-start | bytes 393224 | tf_op jit(solution)/shard_map/ppermute | solution.py:27
  73.4 10.3 %collective-permute-start.20 = (f32[2,128,128]{2,1,0:T(8,128)}, f32[2,128,128]{2,1,0:T(8,128)S(1)}, u32[]{:S(2)}, u32[]{:S(2)}) collective-permute-start(f32[2,128,128]{2,1,0:T(8,128)} %get-tuple-element.40), channel_id=1, source_target_pairs={{0,5},{1,6},{2,7},{3,4},{4,9},{5,10},{6,11},{7,8},{8,13},{9,14},{1... | collective-permute-start | bytes 393224 | tf_op jit(solution)/shard_map/ppermute | solution.py:27
  75.4 10.8 %collective-permute-start.21 = (f32[2,128,128]{2,1,0:T(8,128)S(1)}, f32[2,128,128]{2,1,0:T(8,128)S(1)}, u32[]{:S(2)}, u32[]{:S(2)}) collective-permute-start(f32[2,128,128]{2,1,0:T(8,128)S(1)} %copy-done.33), channel_id=1, source_target_pairs={{0,1},{1,2},{2,3},{3,0},{4,5},{5,6},{6,7},{7,4},{8,9},{9,10},{10,1... | collective-permute-start | bytes 393224 | tf_op jit(solution)/shard_map/ppermute | solution.py:27
  76.3 9.9 %collective-permute-start.22 = (f32[2,128,128]{2,1,0:T(8,128)S(1)}, f32[2,128,128]{2,1,0:T(8,128)S(1)}, u32[]{:S(2)}, u32[]{:S(2)}) collective-permute-start(f32[2,128,128]{2,1,0:T(8,128)S(1)} %copy-done.31), channel_id=1, source_target_pairs={{0,4},{1,5},{2,6},{3,7},{4,8},{5,9},{6,10},{7,11},{8,12},{9,13},{1... | collective-permute-start | bytes 393224 | tf_op jit(solution)/shard_map/ppermute | solution.py:27
  81.8 8.0 %collective-permute-start.23 = (f32[2,128,128]{2,1,0:T(8,128)S(1)}, f32[2,128,128]{2,1,0:T(8,128)S(1)}, u32[]{:S(2)}, u32[]{:S(2)}) collective-permute-start(f32[2,128,128]{2,1,0:T(8,128)S(1)} %copy-done.30), channel_id=1, source_target_pairs={{0,5},{1,6},{2,7},{3,4},{4,9},{5,10},{6,11},{7,8},{8,13},{9,14},{1... | collective-permute-start | bytes 393224 | tf_op jit(solution)/shard_map/ppermute | solution.py:27
  (34 other events, 140.2 us)
where the time goes:
time: 94.3 us; the launch traced here: 93.9 us
  Pallas kernels  37.2 us (39%)
  waiting for transfers between devices  24 us (25%)
  starting transfers between devices  22.4 us (24%)
  local copies, waits for them, and re-layouts  7.72 us (8%)
  other arithmetic  1.62 us (2%)
    pallas_call x11, Pallas kernels, call(): pl.pallas_call(kernel, out_shape=outs, in_specs=ins, out_specs=[VMEM] * l...  37.2 us
    ppermute x24, waiting for transfers between devices, moved(): return lax.ppermute(value, ('row', 'col'), pairs)  24 us
    ppermute x24, starting transfers between devices, moved(): return lax.ppermute(value, ('row', 'col'), pairs)  22.4 us
    unnamed x69, local copies, waits for them, and re-layouts  6.08 us
  transfers between devices with their start and end apart: 24, of which 7 were waited for; matrix products, arithmetic and copies ran while one was open for 1% of the time, Pallas kernels for 18%

commit v1 on v0

--- a/solution.py
+++ b/solution.py
@@ -10,6 +10,8 @@
 from jax.sharding import PartitionSpec as P
 
 ITERS = 2
+VLIM = 24 * 2**20
+FUSED = True
 step_rate = 0.02
 F32 = jnp.float32
 BF16 = jnp.bfloat16
@@ -17,12 +19,13 @@
 SMEM = pl.BlockSpec(memory_space=pltpu.SMEM)
 
 
-def moved(value, rows, cols):
+def moved(value, rows, cols, parity=None):
     nr, nc = lax.axis_size("row"), lax.axis_size("col")
     pairs = [
         (r * nc + c, ((r + rows) % nr) * nc + (c + cols) % nc)
         for r in range(nr)
         for c in range(nc)
+        if parity is None or r % 2 == parity
     ]
     return lax.ppermute(value, ("row", "col"), pairs)
 
@@ -38,7 +41,7 @@
         high = table.astype(ml_dtypes.bfloat16)
         low = (table - high.astype(np.float32)).astype(ml_dtypes.bfloat16)
         tables += [high, low]
-    return [jnp.asarray(t) for t in tables]
+    return jnp.asarray(np.stack(tables))
 
 
 def halves(x):
@@ -109,7 +112,9 @@
                 ref[part] += value
 
 
-def prepare_kernel(positions, probe, phase, rolled, prop):
+def prepare_kernel(positions, probe, phase, measured, constants, rolled, prop, intensity, tables):
+    tables[...] = constants[...]
+    intensity[...] = measured[...]
     for slot in range(rolled.shape[0]):
         for part in range(2):
             x = pltpu.roll(probe[part], positions[2 * slot], 0)
@@ -118,8 +123,8 @@
     prop[1] = jnp.sin(phase[...])
 
 
-def first_slice_kernel(positions, rolled, t00, t01, t10, t11, prop, rh, rl, lh, ll, wave):
-    right, left = (rh[...], rl[...]), (lh[...], ll[...])
+def first_slice_kernel(positions, rolled, t00, t01, t10, t11, prop, tables, wave):
+    right, left = (tables[0], tables[1]), (tables[2], tables[3])
     width = prop.shape[-1]
     tiles = (t00, t01, t10, t11)
     h = (prop[0], prop[1])
@@ -137,9 +142,9 @@
 
 
 def second_slice_kernel(
-    positions, counts, wave, t00, t01, t10, t11, measured, rh, rl, lh, ll, g00, g01, g10, g11, back
+    positions, counts, wave, t00, t01, t10, t11, measured, tables, g00, g01, g10, g11, back
 ):
-    right, left = (rh[...], rl[...]), (lh[...], ll[...])
+    right, left = (tables[0], tables[1]), (tables[2], tables[3])
     width = measured.shape[-1]
     tiles = (t00, t01, t10, t11)
     for pair in range(0, wave.shape[0], 2):
@@ -169,8 +174,8 @@
             back[slot, 0], back[slot, 1] = times_conj(g[k], w)
 
 
-def first_back_kernel(positions, back, rolled, prop, rh, rl, lh, ll, g00, g01, g10, g11):
-    right, left = (rh[...], rl[...]), (lh[...], ll[...])
+def first_back_kernel(positions, back, rolled, prop, tables, g00, g01, g10, g11):
+    right, left = (tables[0], tables[1]), (tables[2], tables[3])
     width = prop.shape[-1]
     h = (prop[0], prop[1])
     for pair in range(0, rolled.shape[0], 2):
@@ -189,18 +194,39 @@
             )
 
 
-def update_kernel(tile, own, right, below, corner, out):
-    out[...] = tile[...] - step_rate * (own[...] + right[...] + below[...] + corner[...])
-
-
-def call(kernel, ins, outs, args, name):
+def add_kernel(a, b, out):
+    out[...] = a[...] + b[...]
+
+
+def update_kernel(tile, own, right, below, out):
+    out[...] = tile[...] - step_rate * (own[...] + right[...] + below[...])
+
+
+def last_kernel(*refs):
+    *ins, out = refs
+    update_kernel(*ins[:4], out.at[0])
+    update_kernel(*ins[4:], out.at[1])
+
+
+def call(kernel, ins, outs, args, name, scratch=()):
     return pl.pallas_call(
         kernel,
         out_shape=outs,
         in_specs=ins,
         out_specs=[VMEM] * len(outs) if isinstance(outs, (list, tuple)) else VMEM,
         name=name,
+        scratch_shapes=scratch,
+        compiler_params=pltpu.CompilerParams(vmem_limit_bytes=VLIM),
     )(*args)
+
+
+def second_back_kernel(
+    positions, counts, rolled, prop, wave, t00, t01, t10, t11, measured, tables, g00, g01, g10, g11, h00, h01, h10, h11, back
+):
+    second_slice_kernel(
+        positions, counts, wave, t00, t01, t10, t11, measured, tables, g00, g01, g10, g11, back
+    )
+    first_back_kernel(positions, back, rolled, prop, tables, h00, h01, h10, h11)
 
 
 def per_device(object_slices, probe, phase, positions, counts, measured):
@@ -213,50 +239,72 @@
     tables = dft_tables(width)
     plane = jax.ShapeDtypeStruct((2, width, width), F32)
     stack = jax.ShapeDtypeStruct((slots, 2, width, width), F32)
-
-    rolled, prop = call(
-        prepare_kernel, [SMEM, VMEM, VMEM], [stack, plane], (corners, probe, phase), "prepare"
-    )
-
-    def fetch(tile):
-        return tile, moved(tile, 0, -1), moved(tile, -1, 0), moved(tile, -1, -1)
+    like = lambda x: jax.ShapeDtypeStruct(x.shape, x.dtype)
+
+    rolled, prop, intensity, tables = call(
+        prepare_kernel,
+        [SMEM] + [VMEM] * 4,
+        [stack, plane, like(intensity), like(tables)],
+        (corners, probe, phase, intensity, tables),
+        "prepare",
+    )
+
+    def fetch(tile, after=None):
+        right = moved(tile, 0, -1)
+        below = moved(tile, -1, 0)
+        if after is not None:
+            right, _ = lax.optimization_barrier((right, after))
+        return tile, right, below, moved(right, -1, 0)
 
     def returned(g):
-        return g[0], moved(g[1], 0, 1), moved(g[2], 1, 0), moved(g[3], 1, 1)
-
-    def update(tile, g):
-        return call(update_kernel, [VMEM] * 5, plane, (tile, *g), "update")
+        near = moved(g[3], 1, 0)
+        low = moved(g[2], 1, 0)
+        side = call(add_kernel, [VMEM] * 2, plane, (g[1], near), "side")
+        return g[0], moved(side, 0, 1), low
 
     first, second = object_slices[0], object_slices[1]
-    for _ in range(ITERS):
+    for step in range(ITERS):
         tiles0 = fetch(first)
-        tiles1 = fetch(second)
+        tiles1 = fetch(second, rolled if step == 0 else None)
         wave = call(
             first_slice_kernel,
-            [SMEM] + [VMEM] * 10,
+            [SMEM] + [VMEM] * 7,
             stack,
-            (corners, rolled, *tiles0, prop, *tables),
+            (corners, rolled, *tiles0, prop, tables),
             "first",
         )
-        *g1, back = call(
-            second_slice_kernel,
-            [SMEM] * 2 + [VMEM] * 10,
-            [plane] * 4 + [stack],
-            (corners, live, wave, *tiles1, intensity, *tables),
-            "second",
-        )
+        if FUSED:
+            *g, _ = call(
+                second_back_kernel,
+                [SMEM] * 2 + [VMEM] * 9,
+                [plane] * 8 + [stack],
+                (corners, live, rolled, prop, wave, *tiles1, intensity, tables),
+                "second_back",
+            )
+            g1, g0 = g[:4], g[4:]
+        else:
+            *g1, back = call(
+                second_slice_kernel,
+                [SMEM] * 2 + [VMEM] * 7,
+                [plane] * 4 + [stack],
+                (corners, live, wave, *tiles1, intensity, tables),
+                "second",
+            )
+            g0 = call(
+                first_back_kernel,
+                [SMEM] + [VMEM] * 4,
+                [plane] * 4,
+                (corners, back, rolled, prop, tables),
+                "back",
+            )
         g1 = returned(g1)
-        g0 = call(
-            first_back_kernel,
-            [SMEM] + [VMEM] * 7,
-            [plane] * 4,
-            (corners, back, rolled, prop, *tables),
-            "back",
-        )
         g0 = returned(g0)
-        second = update(second, g1)
-        first = update(first, g0)
-    return jnp.stack([first, second])
+        if step + 1 < ITERS:
+            second = call(update_kernel, [VMEM] * 4, plane, (second, *g1), "update")
+            first = call(update_kernel, [VMEM] * 4, plane, (first, *g0), "update")
+    return call(
+        last_kernel, [VMEM] * 8, like(object_slices), (first, *g0, second, *g1), "last"
+    )
 
 
 def solution(mesh):

time: 94.3 us -> 68.2 us (0.72)
  Pallas kernels: 37.2 us -> 18.3 us
  local copies, waits for them, and re-layouts: 7.72 us -> 3.93 us
  starting transfers between devices: 22.4 us -> 19 us
  waiting for transfers between devices: 24 us -> 25.9 us
  other arithmetic: 1.62 us -> 0 us
    pallas_call x11 -> x12, Pallas kernels: 37.2 us -> 18.3 us  [call(): pl.pallas_call(kernel, out_shape=outs, in_specs=ins, out_specs=[VMEM] * l...]
    ppermute x24, starting transfers between devices: 22.4 us -> 19 us  [moved(): return lax.ppermute(value, ('row', 'col'), pairs)]
    unnamed x69 -> x11, local copies, waits for them, and re-layouts: 6.08 us -> 2.8 us
    ppermute x24, waiting for transfers between devices: 24 us -> 25.9 us  [moved(): return lax.ppermute(value, ('row', 'col'), pairs)]
    another operation x1 -> x0, other arithmetic: 1.62 us -> none  [per_device(): return jnp.stack([first, second])]
  transfers between devices with their start and end apart: 24 -> 24, of which waited for: 7 -> 13; matrix products, arithmetic and copies ran while one was open for 1% -> 0% of each run, Pallas kernels for 18% -> 10%
where the time goes in v1:
time: 68.2 us; the launch traced here: 68 us
  waiting for transfers between devices  25.9 us (38%)
  starting transfers between devices  19 us (28%)
  Pallas kernels  18.3 us (27%)
  local copies, waits for them, and re-layouts  3.93 us (6%)
  between operations  0.82 us (1%)
    ppermute x24, waiting for transfers between devices, moved(): return lax.ppermute(value, ('row', 'col'), pairs)  25.9 us
    ppermute x24, starting transfers between devices, moved(): return lax.ppermute(value, ('row', 'col'), pairs)  19 us
    pallas_call x12, Pallas kernels, call(): pl.pallas_call(kernel, out_shape=outs, in_specs=ins, out_specs=[VMEM] * l...  18.3 us
    unnamed x11, local copies, waits for them, and re-layouts  2.8 us
  transfers between devices with their start and end apart: 24, of which 13 were waited for; matrix products, arithmetic and copies ran while one was open for 0% of the time, Pallas kernels for 10%

profile of v1, /device:TPU:0, one launch (start us, length us, event | category | flops | bytes accessed | tf_op | source)
XLA Modules:
  0.0 68.0 jit_solution(11365208486044605200)
XLA Ops:
  0.0 1.0 %slice_bitcast_fusion = (f32[2,128,128]{2,1,0:T(8,128)S(1)}, f32[2,128,128]{2,1,0:T(8,128)S(1)}) fusion(f32[2,2,128,128]{3,2,1,0:T(8,128)} %param.7), kind=kLoop, calls=%fused_computation | loop fusion | bytes 524288 | tf_op jit(solution)/shard_map/squeeze | solution.py:265
  1.1 5.1 %collective-permute-start = (f32[2,128,128]{2,1,0:T(8,128)S(1)}, f32[2,128,128]{2,1,0:T(8,128)S(1)}, u32[]{:S(2)}, u32[]{:S(2)}) collective-permute-start(f32[2,128,128]{2,1,0:T(8,128)S(1)} %get-tuple-element.48.t00.tile), channel_id=1, source_target_pairs={{0,3},{1,0},{2,1},{3,2},{4,7},{5,4},{6,5},{7,6},{8,11},{9,8},{10,9... | collective-permute-start | bytes 393224 | tf_op jit(solution)/shard_map/ppermute | solution.py:30
  6.6 1.3 %collective-permute-start.4 = (f32[2,128,128]{2,1,0:T(8,128)S(1)}, f32[2,128,128]{2,1,0:T(8,128)S(1)}, u32[]{:S(2)}, u32[]{:S(2)}) collective-permute-start(f32[2,128,128]{2,1,0:T(8,128)S(1)} %get-tuple-element.47.t00.tile), channel_id=1, source_target_pairs={{0,28},{1,29},{2,30},{3,31},{4,0},{5,1},{6,2},{7,3},{8,4},{9,5},{1... | collective-permute-start | bytes 393224 | tf_op jit(solution)/shard_map/ppermute | solution.py:30
  8.0 1.2 %collective-permute-start.1 = (f32[2,128,128]{2,1,0:T(8,128)S(1)}, f32[2,128,128]{2,1,0:T(8,128)S(1)}, u32[]{:S(2)}, u32[]{:S(2)}) collective-permute-start(f32[2,128,128]{2,1,0:T(8,128)S(1)} %get-tuple-element.48.t00.tile), channel_id=1, source_target_pairs={{0,28},{1,29},{2,30},{3,31},{4,0},{5,1},{6,2},{7,3},{8,4},{9,5},{1... | collective-permute-start | bytes 393224 | tf_op jit(solution)/shard_map/ppermute | solution.py:30
  12.1 1.1 %prepare.1 = (f32[4,2,128,128]{3,2,1,0:T(8,128)S(1)}, f32[2,128,128]{2,1,0:T(8,128)S(1)}, f32[4,128,128]{2,1,0:T(8,128)S(1)}, bf16[4,256,256]{2,1,0:T(8,128)(2,1)S(1)}) custom-call(s32[8]{0:T(128)S(1)} %reshape.6.positions, f32[2,128,128]{2,1,0:T(8,128)S(1)} %copy-done.2, f32[128,128]{1,0:T(8,128)S(1)} %copy-done.3, f32[4,128,128]{2,1,0:T(8,128)S(1)} %bitcast.8, ...), custom_call_target="tpu_custom_call" | custom-call | tf_op jit(solution)/shard_map/prepare/pallas_call | solution.py:212
  14.6 1.2 %collective-permute-done.2.t11 = f32[2,128,128]{2,1,0:T(8,128)S(1)} collective-permute-done((f32[2,128,128]{2,1,0:T(8,128)S(1)}, f32[2,128,128]{2,1,0:T(8,128)S(1)}, u32[]{:S(2)}, u32[]{:S(2)}) %collective-permute-start.2) | collective-permute-done | bytes 131104 | tf_op jit(solution)/shard_map/ppermute | solution.py:30
  15.8 2.8 %first.2.wave = f32[4,2,128,128]{3,2,1,0:T(8,128)S(1)} custom-call(s32[8]{0:T(128)S(1)} %reshape.6.positions, f32[4,2,128,128]{3,2,1,0:T(8,128)S(1)} %get-tuple-element.26.rolled, f32[2,128,128]{2,1,0:T(8,128)S(1)} %get-tuple-element.48.t00.tile, f32[2,128,128]{2,1,0:T(8,128)S(1)} %collective-permute-done.t01, ...), custom_call_target="tpu_custom_call" | custom-call | tf_op jit(solution)/shard_map/first/pallas_call | solution.py:212
  18.6 5.4 %second_back.2 = (f32[2,128,128]{2,1,0:T(8,128)S(1)}, f32[2,128,128]{2,1,0:T(8,128)S(1)}, f32[2,128,128]{2,1,0:T(8,128)S(1)}, f32[2,128,128]{2,1,0:T(8,128)S(1)}...) custom-call(s32[8]{0:T(128)S(1)} %reshape.6.positions, ...), custom_call_target="tpu_custom_call" | custom-call | tf_op jit(solution)/shard_map/second_back/pallas_call | solution.py:212
  24.0 1.1 %collective-permute-start.6 = (f32[2,128,128]{2,1,0:T(8,128)S(1)}, f32[2,128,128]{2,1,0:T(8,128)S(1)}, u32[]{:S(2)}, u32[]{:S(2)}) collective-permute-start(f32[2,128,128]{2,1,0:T(8,128)S(1)} %get-tuple-element.33), channel_id=1, source_target_pairs={{0,4},{1,5},{2,6},{3,7},{4,8},{5,9},{6,10},{7,11},{8,12},{9,13},{1... | collective-permute-start | bytes 393224 | tf_op jit(solution)/shard_map/ppermute | solution.py:30
  25.1 1.2 %collective-permute-start.8 = (f32[2,128,128]{2,1,0:T(8,128)S(1)}, f32[2,128,128]{2,1,0:T(8,128)S(1)}, u32[]{:S(2)}, u32[]{:S(2)}) collective-permute-start(f32[2,128,128]{2,1,0:T(8,128)S(1)} %get-tuple-element.34), channel_id=1, source_target_pairs={{0,4},{1,5},{2,6},{3,7},{4,8},{5,9},{6,10},{7,11},{8,12},{9,13},{1... | collective-permute-start | bytes 393224 | tf_op jit(solution)/shard_map/ppermute | solution.py:30
  26.3 3.1 %collective-permute-done.6.b = f32[2,128,128]{2,1,0:T(8,128)S(1)} collective-permute-done((f32[2,128,128]{2,1,0:T(8,128)S(1)}, f32[2,128,128]{2,1,0:T(8,128)S(1)}, u32[]{:S(2)}, u32[]{:S(2)}) %collective-permute-start.6) | collective-permute-done | bytes 131104 | tf_op jit(solution)/shard_map/ppermute | solution.py:30
  29.4 1.6 %collective-permute-start.7 = (f32[2,128,128]{2,1,0:T(8,128)S(1)}, f32[2,128,128]{2,1,0:T(8,128)S(1)}, u32[]{:S(2)}, u32[]{:S(2)}) collective-permute-start(f32[2,128,128]{2,1,0:T(8,128)S(1)} %side.4), channel_id=1, source_target_pairs={{0,1},{1,2},{2,3},{3,0},{4,5},{5,6},{6,7},{7,4},{8,9},{9,10},{10,1... | collective-permute-start | bytes 393224 | tf_op jit(solution)/shard_map/ppermute | solution.py:30
  31.1 1.4 %collective-permute-start.13 = (f32[2,128,128]{2,1,0:T(8,128)S(1)}, f32[2,128,128]{2,1,0:T(8,128)S(1)}, u32[]{:S(2)}, u32[]{:S(2)}) collective-permute-start(f32[2,128,128]{2,1,0:T(8,128)S(1)} %side.5), channel_id=1, source_target_pairs={{0,1},{1,2},{2,3},{3,0},{4,5},{5,6},{6,7},{7,4},{8,9},{9,10},{10,1... | collective-permute-start | bytes 393224 | tf_op jit(solution)/shard_map/ppermute | solution.py:30
  32.5 4.5 %collective-permute-done.7.right = f32[2,128,128]{2,1,0:T(8,128)S(1)} collective-permute-done((f32[2,128,128]{2,1,0:T(8,128)S(1)}, f32[2,128,128]{2,1,0:T(8,128)S(1)}, u32[]{:S(2)}, u32[]{:S(2)}) %collective-permute-start.7) | collective-permute-done | bytes 131104 | tf_op jit(solution)/shard_map/ppermute | solution.py:30
  37.1 2.6 %collective-permute-done.13.right = f32[2,128,128]{2,1,0:T(8,128)S(1)} collective-permute-done((f32[2,128,128]{2,1,0:T(8,128)S(1)}, f32[2,128,128]{2,1,0:T(8,128)S(1)}, u32[]{:S(2)}, u32[]{:S(2)}) %collective-permute-start.13) | collective-permute-done | bytes 131104 | tf_op jit(solution)/shard_map/ppermute | solution.py:30
  40.6 2.3 %collective-permute-done.9.t01 = f32[2,128,128]{2,1,0:T(8,128)S(1)} collective-permute-done((f32[2,128,128]{2,1,0:T(8,128)S(1)}, f32[2,128,128]{2,1,0:T(8,128)S(1)}, u32[]{:S(2)}, u32[]{:S(2)}) %collective-permute-start.9) | collective-permute-done | bytes 131104 | tf_op jit(solution)/shard_map/ppermute | solution.py:30
  42.8 2.0 %collective-permute-done.15.t01 = f32[2,128,128]{2,1,0:T(8,128)S(1)} collective-permute-done((f32[2,128,128]{2,1,0:T(8,128)S(1)}, f32[2,128,128]{2,1,0:T(8,128)S(1)}, u32[]{:S(2)}, u32[]{:S(2)}) %collective-permute-start.15) | collective-permute-done | bytes 131104 | tf_op jit(solution)/shard_map/ppermute | solution.py:30
  45.4 2.8 %first.3.wave = f32[4,2,128,128]{3,2,1,0:T(8,128)S(1)} custom-call(s32[8]{0:T(128)S(1)} %reshape.6.positions, f32[4,2,128,128]{3,2,1,0:T(8,128)S(1)} %get-tuple-element.26.rolled, f32[2,128,128]{2,1,0:T(8,128)S(1)} %update.2.t00.refs_0_, f32[2,128,128]{2,1,0:T(8,128)S(1)} %collective-permute-done.9.t01, f32[2,128,128]{2,1,0:T(8,128)S(1)} %collective-permute-done.10.t10, ...), custom_call_target="tpu_custom_call" | custom-call | tf_op jit(solution)/shard_map/first/pallas_call | solution.py:212
  48.2 5.3 %second_back.3 = (f32[2,128,128]{2,1,0:T(8,128)S(1)}, f32[2,128,128]{2,1,0:T(8,128)S(1)}, f32[2,128,128]{2,1,0:T(8,128)S(1)}, f32[2,128,128]{2,1,0:T(8,128)S(1)}...) custom-call(s32[8]{0:T(128)S(1)} %reshape.6.positions, ...), custom_call_target="tpu_custom_call" | custom-call | tf_op jit(solution)/shard_map/second_back/pallas_call | solution.py:212
  54.5 1.3 %collective-permute-start.20 = (f32[2,128,128]{2,1,0:T(8,128)S(1)}, f32[2,128,128]{2,1,0:T(8,128)S(1)}, u32[]{:S(2)}, u32[]{:S(2)}) collective-permute-start(f32[2,128,128]{2,1,0:T(8,128)S(1)} %get-tuple-element.42), channel_id=1, source_target_pairs={{0,4},{1,5},{2,6},{3,7},{4,8},{5,9},{6,10},{7,11},{8,12},{9,13},{1... | collective-permute-start | bytes 393224 | tf_op jit(solution)/shard_map/ppermute | solution.py:30
  55.8 3.1 %collective-permute-done.18.b = f32[2,128,128]{2,1,0:T(8,128)S(1)} collective-permute-done((f32[2,128,128]{2,1,0:T(8,128)S(1)}, f32[2,128,128]{2,1,0:T(8,128)S(1)}, u32[]{:S(2)}, u32[]{:S(2)}) %collective-permute-start.18) | collective-permute-done | bytes 131104 | tf_op jit(solution)/shard_map/ppermute | solution.py:30
  61.7 1.4 %collective-permute-done.23.refs_7_ = f32[2,128,128]{2,1,0:T(8,128)S(1)} collective-permute-done((f32[2,128,128]{2,1,0:T(8,128)S(1)}, f32[2,128,128]{2,1,0:T(8,128)S(1)}, u32[]{:S(2)}, u32[]{:S(2)}) %collective-permute-start.23) | collective-permute-done | bytes 131104 | tf_op jit(solution)/shard_map/ppermute | solution.py:30
  63.1 2.6 %collective-permute-done.19.refs_2_ = f32[2,128,128]{2,1,0:T(8,128)S(1)} collective-permute-done((f32[2,128,128]{2,1,0:T(8,128)S(1)}, f32[2,128,128]{2,1,0:T(8,128)S(1)}, u32[]{:S(2)}, u32[]{:S(2)}) %collective-permute-start.19) | collective-permute-done | bytes 131104 | tf_op jit(solution)/shard_map/ppermute | solution.py:30
  65.8 1.4 %collective-permute-done.22.refs_6_ = f32[2,128,128]{2,1,0:T(8,128)S(1)} collective-permute-done((f32[2,128,128]{2,1,0:T(8,128)S(1)}, f32[2,128,128]{2,1,0:T(8,128)S(1)}, u32[]{:S(2)}, u32[]{:S(2)}) %collective-permute-start.22) | collective-permute-done | bytes 131104 | tf_op jit(solution)/shard_map/ppermute | solution.py:30
  (49 shorter events, 10.1 us)
Async XLA Ops:
  1.1 12.1 %collective-permute-start = (f32[2,128,128]{2,1,0:T(8,128)S(1)}, f32[2,128,128]{2,1,0:T(8,128)S(1)}, u32[]{:S(2)}, u32[]{:S(2)}) collective-permute-start(f32[2,128,128]{2,1,0:T(8,128)S(1)} %get-tuple-element.48.t00.tile), channel_id=1, source_target_pairs={{0,3},{1,0},{2,1},{3,2},{4,7},{5,4},{6,5},{7,6},{8,11},{9,8},{10,9... | collective-permute-start | bytes 393224 | tf_op jit(solution)/shard_map/ppermute | solution.py:30
  6.2 7.1 %collective-permute-start.3 = (f32[2,128,128]{2,1,0:T(8,128)S(1)}, f32[2,128,128]{2,1,0:T(8,128)S(1)}, u32[]{:S(2)}, u32[]{:S(2)}) collective-permute-start(f32[2,128,128]{2,1,0:T(8,128)S(1)} %get-tuple-element.47.t00.tile), channel_id=1, source_target_pairs={{0,3},{1,0},{2,1},{3,2},{4,7},{5,4},{6,5},{7,6},{8,11},{9,8},{10,9... | collective-permute-start | bytes 393224 | tf_op jit(solution)/shard_map/ppermute | solution.py:30
  6.6 11.9 %collective-permute-start.4 = (f32[2,128,128]{2,1,0:T(8,128)S(1)}, f32[2,128,128]{2,1,0:T(8,128)S(1)}, u32[]{:S(2)}, u32[]{:S(2)}) collective-permute-start(f32[2,128,128]{2,1,0:T(8,128)S(1)} %get-tuple-element.47.t00.tile), channel_id=1, source_target_pairs={{0,28},{1,29},{2,30},{3,31},{4,0},{5,1},{6,2},{7,3},{8,4},{9,5},{1... | collective-permute-start | bytes 393224 | tf_op jit(solution)/shard_map/ppermute | solution.py:30
  8.0 6.6 %collective-permute-start.1 = (f32[2,128,128]{2,1,0:T(8,128)S(1)}, f32[2,128,128]{2,1,0:T(8,128)S(1)}, u32[]{:S(2)}, u32[]{:S(2)}) collective-permute-start(f32[2,128,128]{2,1,0:T(8,128)S(1)} %get-tuple-element.48.t00.tile), channel_id=1, source_target_pairs={{0,28},{1,29},{2,30},{3,31},{4,0},{5,1},{6,2},{7,3},{8,4},{9,5},{1... | collective-permute-start | bytes 393224 | tf_op jit(solution)/shard_map/ppermute | solution.py:30
  13.2 2.6 %collective-permute-start.2 = (f32[2,128,128]{2,1,0:T(8,128)S(1)}, f32[2,128,128]{2,1,0:T(8,128)S(1)}, u32[]{:S(2)}, u32[]{:S(2)}) collective-permute-start(f32[2,128,128]{2,1,0:T(8,128)S(1)} %collective-permute-done.t01), channel_id=1, source_target_pairs={{0,28},{1,29},{2,30},{3,31},{4,0},{5,1},{6,2},{7,3},{8,4},{9,5},{1... | collective-permute-start | bytes 393224 | tf_op jit(solution)/shard_map/ppermute | solution.py:30
  13.3 5.3 %collective-permute-start.5 = (f32[2,128,128]{2,1,0:T(8,128)S(1)}, f32[2,128,128]{2,1,0:T(8,128)S(1)}, u32[]{:S(2)}, u32[]{:S(2)}) collective-permute-start(f32[2,128,128]{2,1,0:T(8,128)S(1)} %collective-permute-done.3.t01), channel_id=1, source_target_pairs={{0,28},{1,29},{2,30},{3,31},{4,0},{5,1},{6,2},{7,3},{8,4},{9,5},{1... | collective-permute-start | bytes 393224 | tf_op jit(solution)/shard_map/ppermute | solution.py:30
  24.0 5.4 %collective-permute-start.6 = (f32[2,128,128]{2,1,0:T(8,128)S(1)}, f32[2,128,128]{2,1,0:T(8,128)S(1)}, u32[]{:S(2)}, u32[]{:S(2)}) collective-permute-start(f32[2,128,128]{2,1,0:T(8,128)S(1)} %get-tuple-element.33), channel_id=1, source_target_pairs={{0,4},{1,5},{2,6},{3,7},{4,8},{5,9},{6,10},{7,11},{8,12},{9,13},{1... | collective-permute-start | bytes 393224 | tf_op jit(solution)/shard_map/ppermute | solution.py:30
  25.1 5.9 %collective-permute-start.12 = (f32[2,128,128]{2,1,0:T(8,128)S(1)}, f32[2,128,128]{2,1,0:T(8,128)S(1)}, u32[]{:S(2)}, u32[]{:S(2)}) collective-permute-start(f32[2,128,128]{2,1,0:T(8,128)S(1)} %get-tuple-element.37), channel_id=1, source_target_pairs={{0,4},{1,5},{2,6},{3,7},{4,8},{5,9},{6,10},{7,11},{8,12},{9,13},{1... | collective-permute-start | bytes 393224 | tf_op jit(solution)/shard_map/ppermute | solution.py:30
  25.1 7.3 %collective-permute-start.8 = (f32[2,128,128]{2,1,0:T(8,128)S(1)}, f32[2,128,128]{2,1,0:T(8,128)S(1)}, u32[]{:S(2)}, u32[]{:S(2)}) collective-permute-start(f32[2,128,128]{2,1,0:T(8,128)S(1)} %get-tuple-element.34), channel_id=1, source_target_pairs={{0,4},{1,5},{2,6},{3,7},{4,8},{5,9},{6,10},{7,11},{8,12},{9,13},{1... | collective-permute-start | bytes 393224 | tf_op jit(solution)/shard_map/ppermute | solution.py:30
  29.4 7.6 %collective-permute-start.7 = (f32[2,128,128]{2,1,0:T(8,128)S(1)}, f32[2,128,128]{2,1,0:T(8,128)S(1)}, u32[]{:S(2)}, u32[]{:S(2)}) collective-permute-start(f32[2,128,128]{2,1,0:T(8,128)S(1)} %side.4), channel_id=1, source_target_pairs={{0,1},{1,2},{2,3},{3,0},{4,5},{5,6},{6,7},{7,4},{8,9},{9,10},{10,1... | collective-permute-start | bytes 393224 | tf_op jit(solution)/shard_map/ppermute | solution.py:30
  31.1 6.0 %collective-permute-start.14 = (f32[2,128,128]{2,1,0:T(8,128)S(1)}, f32[2,128,128]{2,1,0:T(8,128)S(1)}, u32[]{:S(2)}, u32[]{:S(2)}) collective-permute-start(f32[2,128,128]{2,1,0:T(8,128)S(1)} %get-tuple-element.38), channel_id=1, source_target_pairs={{0,4},{1,5},{2,6},{3,7},{4,8},{5,9},{6,10},{7,11},{8,12},{9,13},{1... | collective-permute-start | bytes 393224 | tf_op jit(solution)/shard_map/ppermute | solution.py:30
  31.1 8.6 %collective-permute-start.13 = (f32[2,128,128]{2,1,0:T(8,128)S(1)}, f32[2,128,128]{2,1,0:T(8,128)S(1)}, u32[]{:S(2)}, u32[]{:S(2)}) collective-permute-start(f32[2,128,128]{2,1,0:T(8,128)S(1)} %side.5), channel_id=1, source_target_pairs={{0,1},{1,2},{2,3},{3,0},{4,5},{5,6},{6,7},{7,4},{8,9},{9,10},{10,1... | collective-permute-start | bytes 393224 | tf_op jit(solution)/shard_map/ppermute | solution.py:30
  37.0 5.8 %collective-permute-start.9 = (f32[2,128,128]{2,1,0:T(8,128)S(1)}, f32[2,128,128]{2,1,0:T(8,128)S(1)}, u32[]{:S(2)}, u32[]{:S(2)}) collective-permute-start(f32[2,128,128]{2,1,0:T(8,128)S(1)} %update.2.t00.refs_0_), channel_id=1, source_target_pairs={{0,3},{1,0},{2,1},{3,2},{4,7},{5,4},{6,5},{7,6},{8,11},{9,8},{10,9... | collective-permute-start | bytes 393224 | tf_op jit(solution)/shard_map/ppermute | solution.py:30
  39.7 5.1 %collective-permute-start.15 = (f32[2,128,128]{2,1,0:T(8,128)S(1)}, f32[2,128,128]{2,1,0:T(8,128)S(1)}, u32[]{:S(2)}, u32[]{:S(2)}) collective-permute-start(f32[2,128,128]{2,1,0:T(8,128)S(1)} %update.3.t00.refs_4_), channel_id=1, source_target_pairs={{0,3},{1,0},{2,1},{3,2},{4,7},{5,4},{6,5},{7,6},{8,11},{9,8},{10,9... | collective-permute-start | bytes 393224 | tf_op jit(solution)/shard_map/ppermute | solution.py:30
  39.8 5.1 %collective-permute-start.10 = (f32[2,128,128]{2,1,0:T(8,128)S(1)}, f32[2,128,128]{2,1,0:T(8,128)S(1)}, u32[]{:S(2)}, u32[]{:S(2)}) collective-permute-start(f32[2,128,128]{2,1,0:T(8,128)S(1)} %update.2.t00.refs_0_), channel_id=1, source_target_pairs={{0,28},{1,29},{2,30},{3,31},{4,0},{5,1},{6,2},{7,3},{8,4},{9,5},{1... | collective-permute-start | bytes 393224 | tf_op jit(solution)/shard_map/ppermute | solution.py:30
  42.8 2.5 %collective-permute-start.11 = (f32[2,128,128]{2,1,0:T(8,128)S(1)}, f32[2,128,128]{2,1,0:T(8,128)S(1)}, u32[]{:S(2)}, u32[]{:S(2)}) collective-permute-start(f32[2,128,128]{2,1,0:T(8,128)S(1)} %collective-permute-done.9.t01), channel_id=1, source_target_pairs={{0,28},{1,29},{2,30},{3,31},{4,0},{5,1},{6,2},{7,3},{8,4},{9,5},{1... | collective-permute-start | bytes 393224 | tf_op jit(solution)/shard_map/ppermute | solution.py:30
  42.8 5.3 %collective-permute-start.16 = (f32[2,128,128]{2,1,0:T(8,128)S(1)}, f32[2,128,128]{2,1,0:T(8,128)S(1)}, u32[]{:S(2)}, u32[]{:S(2)}) collective-permute-start(f32[2,128,128]{2,1,0:T(8,128)S(1)} %update.3.t00.refs_4_), channel_id=1, source_target_pairs={{0,28},{1,29},{2,30},{3,31},{4,0},{5,1},{6,2},{7,3},{8,4},{9,5},{1... | collective-permute-start | bytes 393224 | tf_op jit(solution)/shard_map/ppermute | solution.py:30
  44.9 3.3 %collective-permute-start.17 = (f32[2,128,128]{2,1,0:T(8,128)S(1)}, f32[2,128,128]{2,1,0:T(8,128)S(1)}, u32[]{:S(2)}, u32[]{:S(2)}) collective-permute-start(f32[2,128,128]{2,1,0:T(8,128)S(1)} %collective-permute-done.15.t01), channel_id=1, source_target_pairs={{0,28},{1,29},{2,30},{3,31},{4,0},{5,1},{6,2},{7,3},{8,4},{9,5},{1... | collective-permute-start | bytes 393224 | tf_op jit(solution)/shard_map/ppermute | solution.py:30
  53.5 5.4 %collective-permute-start.18 = (f32[2,128,128]{2,1,0:T(8,128)S(1)}, f32[2,128,128]{2,1,0:T(8,128)S(1)}, u32[]{:S(2)}, u32[]{:S(2)}) collective-permute-start(f32[2,128,128]{2,1,0:T(8,128)S(1)} %get-tuple-element.41), channel_id=1, source_target_pairs={{0,4},{1,5},{2,6},{3,7},{4,8},{5,9},{6,10},{7,11},{8,12},{9,13},{1... | collective-permute-start | bytes 393224 | tf_op jit(solution)/shard_map/ppermute | solution.py:30
  54.5 5.9 %collective-permute-start.21 = (f32[2,128,128]{2,1,0:T(8,128)S(1)}, f32[2,128,128]{2,1,0:T(8,128)S(1)}, u32[]{:S(2)}, u32[]{:S(2)}) collective-permute-start(f32[2,128,128]{2,1,0:T(8,128)S(1)} %get-tuple-element.45), channel_id=1, source_target_pairs={{0,4},{1,5},{2,6},{3,7},{4,8},{5,9},{6,10},{7,11},{8,12},{9,13},{1... | collective-permute-start | bytes 393224 | tf_op jit(solution)/shard_map/ppermute | solution.py:30
  54.5 7.3 %collective-permute-start.20 = (f32[2,128,128]{2,1,0:T(8,128)S(1)}, f32[2,128,128]{2,1,0:T(8,128)S(1)}, u32[]{:S(2)}, u32[]{:S(2)}) collective-permute-start(f32[2,128,128]{2,1,0:T(8,128)S(1)} %get-tuple-element.42), channel_id=1, source_target_pairs={{0,4},{1,5},{2,6},{3,7},{4,8},{5,9},{6,10},{7,11},{8,12},{9,13},{1... | collective-permute-start | bytes 393224 | tf_op jit(solution)/shard_map/ppermute | solution.py:30
  55.8 7.4 %collective-permute-start.23 = (f32[2,128,128]{2,1,0:T(8,128)S(1)}, f32[2,128,128]{2,1,0:T(8,128)S(1)}, u32[]{:S(2)}, u32[]{:S(2)}) collective-permute-start(f32[2,128,128]{2,1,0:T(8,128)S(1)} %get-tuple-element.46), channel_id=1, source_target_pairs={{0,4},{1,5},{2,6},{3,7},{4,8},{5,9},{6,10},{7,11},{8,12},{9,13},{1... | collective-permute-start | bytes 393224 | tf_op jit(solution)/shard_map/ppermute | solution.py:30
  58.9 6.8 %collective-permute-start.19 = (f32[2,128,128]{2,1,0:T(8,128)S(1)}, f32[2,128,128]{2,1,0:T(8,128)S(1)}, u32[]{:S(2)}, u32[]{:S(2)}) collective-permute-start(f32[2,128,128]{2,1,0:T(8,128)S(1)} %side.6), channel_id=1, source_target_pairs={{0,1},{1,2},{2,3},{3,0},{4,5},{5,6},{6,7},{7,4},{8,9},{9,10},{10,1... | collective-permute-start | bytes 393224 | tf_op jit(solution)/shard_map/ppermute | solution.py:30
  60.4 6.8 %collective-permute-start.22 = (f32[2,128,128]{2,1,0:T(8,128)S(1)}, f32[2,128,128]{2,1,0:T(8,128)S(1)}, u32[]{:S(2)}, u32[]{:S(2)}) collective-permute-start(f32[2,128,128]{2,1,0:T(8,128)S(1)} %side.7), channel_id=1, source_target_pairs={{0,1},{1,2},{2,3},{3,0},{4,5},{5,6},{6,7},{7,4},{8,9},{9,10},{10,1... | collective-permute-start | bytes 393224 | tf_op jit(solution)/shard_map/ppermute | solution.py:30
  (5 other events, 20.2 us)
